TPU v7x, 32 devices: a whole 2x2x4 slice. The times are simulated.
32 devices in a mesh: pack: 8 (over z, y), ctx: 4 (over x, core).
Axes of the slice: x: 2, y: 2, z: 4, core: 2. Of those that a mesh axis runs over, the one named last changes fastest.
Arguments:
- signals: bfloat16 [4096, 10240], P(('pack', 'ctx')), may hold values from -36 to 36
- state_io: bfloat16 [4096, 256], P(('pack', 'ctx')), may hold values from -0.8984375 to 0.8984375
- step_raw: bfloat16 [4096, 80], P(('pack', 'ctx')), may hold values from -4 to 4
- row_target: int32 [8, 4, 16], P('pack', 'ctx'), may hold values from 0 to 127, as said below
- table_start: int32 [8, 4], P('pack', 'ctx'), may hold values 0 or 1
- log_rate: float32 [80], replicated, may hold values from -11 to -2
- step_bias: float32 [80], replicated, may hold values from -0.5 to 0.5
- skip_gain: float32 [80], replicated, may hold values from 0.5 to 1.5
- norm_gain: float32 [5120], replicated, may hold values from 0.5 to 1.5
Outputs:
- gated: bfloat16 [4096, 5120], P(('pack', 'ctx'))
Inputs may be any that keep to these rules, and one draw needn't show every extreme that they name: With t = row_target[p, c, j], t // 16 is the sequence that takes the row and t % 16 its row slot in slab c of that sequence; every slot of every slab is taken exactly once, and the rows of one device go exactly 2 to each sequence.
All inputs are finite; a program needn't handle non-finite values. No bound on the sum of `table_start` on one device may be relied on, other than what follows from the above.
Results may differ from a plain program's by a relative error of at most 0.0046.
Values may be sent and summed in bfloat16 or wider, within the bound.
A program may use at most 192 MiB of HBM per device.

v0:
```python
import jax
import jax.numpy as jnp
from jax import lax
from jax.sharding import PartitionSpec as P

GROUP = 128
ROW = 8


def passed_along(block, axis, distance):
    devices = range(lax.axis_size(axis))
    route = [(i - distance, i) for i in devices if i - distance in devices]
    return lax.ppermute(block, axis, route)


def body(
    signals, state_io, step_raw, row_target, table_start, log_rate, step_bias, skip_gain, norm_gain
):
    pack_size = lax.axis_size("pack")
    ctx_size = lax.axis_size("ctx")
    row_count = row_target.shape[2]
    capacity = row_count // pack_size
    slot_count = pack_size * capacity
    inner_width = signals.shape[1] // 2
    head_count = log_rate.shape[0]
    head_width = inner_width // head_count
    state_width = state_io.shape[1] // 2
    token_count = row_count * ROW
    groups = token_count // GROUP
    targets = row_target.reshape(row_count)
    destination = targets // row_count
    row_index = jnp.arange(row_count, dtype=jnp.int32)
    earlier_rows = (destination[:, None] == destination[None, :]) & (
        row_index[None, :] < row_index[:, None]
    )
    earlier_count = jnp.sum(earlier_rows.astype(jnp.int32), axis=1)
    position = destination * capacity + earlier_count
    send_match = position[None, :] == jnp.arange(slot_count, dtype=jnp.int32)[:, None]
    filled = jnp.any(send_match, axis=1)
    source_row = jnp.where(
        filled, jnp.sum(jnp.where(send_match, row_index[None, :], 0), axis=1), row_count
    )
    send_slot = jnp.where(
        filled, jnp.sum(jnp.where(send_match, (targets % row_count)[None, :], 0), axis=1), -1
    )

    def outgoing(values):
        blocks = values.reshape(row_count, ROW, values.shape[1])
        return jnp.take(blocks, source_row, axis=0, mode="fill", fill_value=0)

    signal_got, io_got, raw_got, slot_got = (
        lax.all_to_all(
            outgoing(signals[:, inner_width:]), "pack", split_axis=0, concat_axis=0, tiled=True
        ),
        lax.all_to_all(outgoing(state_io), "pack", split_axis=0, concat_axis=0, tiled=True),
        lax.all_to_all(outgoing(step_raw), "pack", split_axis=0, concat_axis=0, tiled=True),
        lax.all_to_all(send_slot, "pack", split_axis=0, concat_axis=0, tiled=True),
    )
    slot_match = slot_got[None, :] == row_index[:, None]
    source_of = jnp.sum(
        jnp.where(slot_match, jnp.arange(slot_count, dtype=jnp.int32)[None, :], 0), axis=1
    )

    def arrange(values):
        return jnp.take(values, source_of, axis=0).reshape(token_count, values.shape[-1])

    signal_in = arrange(signal_got)
    io_rows = arrange(io_got)
    raw_rows = arrange(raw_got)
    inputs = signal_in.reshape(groups, GROUP, head_count, head_width)
    b_proj = io_rows[:, :state_width].reshape(groups, GROUP, state_width)
    c_proj = io_rows[:, state_width:].reshape(groups, GROUP, state_width)
    step_size = jax.nn.softplus(raw_rows.astype(jnp.float32) + step_bias).reshape(
        groups, GROUP, head_count
    )
    log_decay = -jnp.exp(log_rate) * step_size
    cumulative = jnp.cumsum(log_decay, axis=1)
    c_dot_b = jnp.einsum("kin,kjn->kij", c_proj, b_proj, preferred_element_type=jnp.float32)
    causal = jnp.arange(GROUP)[:, None] >= jnp.arange(GROUP)[None, :]
    per_head = cumulative.transpose(0, 2, 1)
    log_gaps = per_head[:, :, :, None] - per_head[:, :, None, :]
    decay_mask = jnp.exp(jnp.where(causal[None, None], log_gaps, -jnp.inf))
    scores = (c_dot_b[:, None] * decay_mask * step_size.transpose(0, 2, 1)[:, :, None, :]).astype(
        jnp.bfloat16
    )
    y_intra = jnp.einsum("khij,kjhp->kihp", scores, inputs, preferred_element_type=jnp.float32)
    to_end = jnp.exp(cumulative[:, -1:, :] - cumulative) * step_size
    weighted = (inputs.astype(jnp.float32) * to_end[..., None]).astype(jnp.bfloat16)
    local_state = jnp.einsum("kjhp,kjn->khpn", weighted, b_proj, preferred_element_type=jnp.float32)
    keep_flag = (1 - table_start.reshape(groups)).astype(jnp.float32)
    group_decay = jnp.exp(cumulative[:, -1, :])
    carry_gain = []
    carry_base = []
    gain_now = keep_flag[0] * jnp.ones((head_count,), jnp.float32)
    base_now = jnp.zeros((head_count, head_width, state_width), jnp.float32)
    for group_id in range(groups):
        if group_id > 0:
            gain_now = keep_flag[group_id] * (group_decay[group_id - 1] * gain_now)
            base_now = keep_flag[group_id] * (
                group_decay[group_id - 1][:, None, None] * base_now + local_state[group_id - 1]
            )
        carry_gain.append(gain_now)
        carry_base.append(base_now)
    leave_gain = group_decay[-1] * gain_now
    leave_base = group_decay[-1][:, None, None] * base_now + local_state[-1]
    incoming = jnp.zeros((head_count, head_width, state_width), jnp.float32)
    for hop_index in range(ctx_size - 1):
        incoming = passed_along(leave_gain[:, None, None] * incoming + leave_base, "ctx", 1)
    entering = jnp.stack(carry_gain)[:, :, None, None] * incoming[None] + jnp.stack(carry_base)
    y_state = jnp.exp(cumulative)[..., None] * jnp.einsum(
        "kin,khpn->kihp", c_proj.astype(jnp.float32), entering, precision=lax.Precision.HIGHEST
    )
    mixed = y_intra + y_state + skip_gain[None, None, :, None] * inputs.astype(jnp.float32)
    mixed = mixed.reshape(token_count, inner_width)
    gate_got = lax.all_to_all(
        outgoing(signals[:, :inner_width]), "pack", split_axis=0, concat_axis=0, tiled=True
    )
    gate_in = arrange(gate_got)
    gated = mixed * jax.nn.silu(gate_in.astype(jnp.float32))
    result = gated * lax.rsqrt(jnp.mean(gated * gated, axis=-1, keepdims=True) + 1e-05) * norm_gain
    return result.astype(jnp.bfloat16)


def solution(mesh):
    return jax.shard_map(
        body,
        mesh=mesh,
        in_specs=(
            P(("pack", "ctx"), None),
            P(("pack", "ctx"), None),
            P(("pack", "ctx"), None),
            P("pack", "ctx", None),
            P("pack", "ctx"),
            P(),
            P(),
            P(),
            P(),
        ),
        out_specs=P(("pack", "ctx"), None),
        check_vma=False,
    )
```

profile of v0, /device:TPU:1, one launch (start us, length us, event | category | flops | bytes accessed | tf_op | source)
XLA Modules:
  0.0 205.0 jit_solution(10574984226833557793)
XLA Ops:
  1.8 6.4 %all-to-all-start.1 = ((s32[8,2,1]{1,2,0:T(1,128)}), s32[8,2,1]{1,2,0:T(1,128)S(1)}, u32[]{:S(2)}, u32[]{:S(2)}) async-start(s32[8,2,1]{1,2,0:T(1,128)} %bitcast.1), calls=%async_computation.1 | async-start | bytes 8192 | tf_op jit(solution)/shard_map/all_to_all | solution.py:57
  13.4 4.8 %all-to-all-start.3 = ((bf16[16,8,80]{2,1,0:T(8,128)(2,1)}), bf16[16,8,80]{2,1,0:T(8,128)(2,1)S(1)}, u32[]{:S(2)}, u32[]{:S(2)}) async-start(bf16[16,8,80]{2,1,0:T(8,128)(2,1)} %broadcast_select_fusion.4), calls=%async_computation.3 | async-start | bytes 65536 | tf_op jit(solution)/shard_map/all_to_all | solution.py:56
  23.8 3.3 %all-to-all-start.2 = ((bf16[16,8,256]{2,1,0:T(8,128)(2,1)}), bf16[16,8,256]{2,1,0:T(8,128)(2,1)S(1)}, u32[]{:S(2)}, u32[]{:S(2)}) async-start(bf16[16,8,256]{2,1,0:T(8,128)(2,1)} %broadcast_select_fusion.3), calls=%async_computation.2 | async-start | bytes 131072 | tf_op jit(solution)/shard_map/all_to_all | solution.py:55
  32.8 4.3 %all-to-all-start = ((bf16[16,8,5120]{2,1,0:T(8,128)(2,1)}), bf16[16,8,5120]{2,1,0:T(8,128)(2,1)}, u32[]{:S(2)}, u32[]{:S(2)}) async-start(bf16[16,8,5120]{2,1,0:T(8,128)(2,1)} %get-tuple-element.23), calls=%async_computation | async-start | bytes 2621440 | tf_op jit(solution)/shard_map/all_to_all | solution.py:52
  39.8 3.6 %mul.205 = f32[128,80,64]{2,1,0:T(8,128)} broadcast(f32[128,80]{1,0:T(8,128)S(1)} %get-tuple-element.18), dimensions={0,1} | broadcast | bytes 2662400 | tf_op jit(solution)/shard_map/mul | solution.py:88
  43.4 4.0 %mul.206 = f32[16,8,5120]{2,1,0:T(8,128)S(1)} reshape(f32[128,80,64]{2,1,0:T(8,128)} %mul.205) | data formatting | bytes 5242880 | tf_op jit(solution)/shard_map/mul | solution.py:88
  48.0 18.1 %all-to-all-done = bf16[16,8,5120]{2,1,0:T(8,128)(2,1)} async-done(((bf16[16,8,5120]{2,1,0:T(8,128)(2,1)}), bf16[16,8,5120]{2,1,0:T(8,128)(2,1)}, u32[]{:S(2)}, u32[]{:S(2)}) %all-to-all-start) | async-done | bytes 1310752 | tf_op jit(solution)/shard_map/all_to_all | solution.py:52
  69.2 3.4 %multiply_convert_fusion.2 = (bf16[16,8,5120]{2,1,0:T(8,128)(2,1)}, bf16[16,8,5120]{2,1,0:T(8,128)(2,1)}) fusion(f32[16,8,5120]{2,1,0:T(8,128)S(1)} %mul.206, bf16[16,8,5120]{2,1,0:T(8,128)(2,1)} %gather_fusion.5, pred[16]{0:T(512)(128)(4,1)S(1)} %compare_and_fusion), kind=kLoop, calls=%fused_computation.28 | loop fusion | flops 2621440 | bytes 6553616 | tf_op jit(solution)/shard_map/convert_element_type | solution.py:88
  72.6 4.4 %convert_element_type.92 = bf16[128,80,64]{2,1,0:T(8,128)(2,1)} reshape(bf16[16,8,5120]{2,1,0:T(8,128)(2,1)} %get-tuple-element.11) | data formatting | bytes 2621440 | tf_op jit(solution)/shard_map/convert_element_type | solution.py:88
  79.7 6.5 %collective-permute-start = (f32[80,64,128]{2,1,0:T(8,128)S(1)}, f32[80,64,128]{2,1,0:T(8,128)S(1)}, u32[]{:S(2)}, u32[]{:S(2)}) collective-permute-start(f32[80,64,128]{2,1,0:T(8,128)S(1)} %get-tuple-element.26), channel_id=1, source_target_pairs={{0,1},{1,2},{2,3},{4,5},{5,6},{6,7},{8,9},{9,10},{10,11},{12,13},{... | collective-permute-start | bytes 7864328 | tf_op jit(solution)/shard_map/ppermute | solution.py:13
  86.2 28.6 %collective-permute-done = f32[80,64,128]{2,1,0:T(8,128)S(1)} collective-permute-done((f32[80,64,128]{2,1,0:T(8,128)S(1)}, f32[80,64,128]{2,1,0:T(8,128)S(1)}, u32[]{:S(2)}, u32[]{:S(2)}) %collective-permute-start) | collective-permute-done | bytes 2621472 | tf_op jit(solution)/shard_map/ppermute | solution.py:13
  116.6 4.4 %collective-permute-start.1 = (f32[80,64,128]{2,1,0:T(8,128)}, f32[80,64,128]{2,1,0:T(8,128)}, u32[]{:S(2)}, u32[]{:S(2)}) collective-permute-start(f32[80,64,128]{2,1,0:T(8,128)} %multiply_add_fusion.1), channel_id=1, source_target_pairs={{0,1},{1,2},{2,3},{4,5},{5,6},{6,7},{8,9},{9,10},{10,11},{12,13},{... | collective-permute-start | bytes 7864328 | tf_op jit(solution)/shard_map/ppermute | solution.py:13
  121.0 4.3 %all-to-all-start.4 = ((bf16[16,8,5120]{2,1,0:T(8,128)(2,1)}), bf16[16,8,5120]{2,1,0:T(8,128)(2,1)}, u32[]{:S(2)}, u32[]{:S(2)}) async-start(bf16[16,8,5120]{2,1,0:T(8,128)(2,1)} %get-tuple-element.22), calls=%async_computation.4 | async-start | bytes 2621440 | tf_op jit(solution)/shard_map/all_to_all | solution.py:115
  125.3 24.6 %collective-permute-done.1 = f32[80,64,128]{2,1,0:T(8,128)} collective-permute-done((f32[80,64,128]{2,1,0:T(8,128)}, f32[80,64,128]{2,1,0:T(8,128)}, u32[]{:S(2)}, u32[]{:S(2)}) %collective-permute-start.1) | collective-permute-done | bytes 2621472 | tf_op jit(solution)/shard_map/ppermute | solution.py:13
  149.9 3.5 %multiply_add_fusion = f32[80,64,128]{2,1,0:T(8,128)} fusion(f32[80,64,128]{2,1,0:T(8,128)} %collective-permute-done.1, f32[80,64,128]{2,1,0:T(8,128)S(1)} %get-tuple-element.27, f32[80]{0:T(128)S(1)} %get-tuple-element.19, f32[80]{0:T(128)S(1)} %get-tuple-element.10), kind=kLoop, calls=%fused_computation.26 | loop fusion | flops 1966080 | bytes 7864960 | tf_op jit(solution)/shard_map/add | solution.py:108
  153.5 4.6 %collective-permute-start.2 = (f32[80,64,128]{2,1,0:T(8,128)}, f32[80,64,128]{2,1,0:T(8,128)}, u32[]{:S(2)}, u32[]{:S(2)}) collective-permute-start(f32[80,64,128]{2,1,0:T(8,128)} %multiply_add_fusion), channel_id=1, source_target_pairs={{0,1},{1,2},{2,3},{4,5},{5,6},{6,7},{8,9},{9,10},{10,11},{12,13},{... | collective-permute-start | bytes 7864328 | tf_op jit(solution)/shard_map/ppermute | solution.py:13
  158.4 4.8 %reshape.606 = f32[1,128,80,64]{3,2,1,0:T(8,128)} reshape(bf16[16,8,5120]{2,1,0:T(8,128)(2,1)} %get-tuple-element.12) | data formatting | bytes 3932160 | tf_op jit(solution)/shard_map/convert_element_type | solution.py:88
  169.6 5.1 %reshape.608 = f32[1,128,80,64]{3,2,1,0:T(8,128)} reshape(f32[16,8,5120]{2,1,0:T(8,128)} %select_convert_fusion) | data formatting | bytes 5242880 | tf_op jit(solution)/shard_map/convert_element_type | solution.py:119
  174.7 6.2 %copy.59 = f32[1,128,80,64]{1,3,2,0:T(8,128)} copy(f32[1,128,80,64]{3,2,1,0:T(8,128)} %reshape.608) | data formatting | bytes 5242880 | tf_op jit(solution)/shard_map/convert_element_type | solution.py:119
  180.9 6.2 %copy.56 = f32[1,128,80,64]{1,3,2,0:T(8,128)} copy(f32[1,128,80,64]{3,2,1,0:T(8,128)} %reshape.606) | data formatting | bytes 5242880 | tf_op jit(solution)/shard_map/convert_element_type | solution.py:88
  187.1 5.4 %fusion = f32[80,64,128]{2,1,0:T(8,128)S(1)} fusion(bf16[128,80,64]{2,1,0:T(8,128)(2,1)} %reshape.601, f32[80,128]{1,0:T(8,128)S(1)} %copy.50, f32[80,128]{1,0:T(8,128)S(1)} %copy.48, f32[128,128]{1,0:T(8,128)S(1)} %fusion.30, pred[128,128]{1,0:T(8,128)(4,1)S(1)} %iota_compare_fusion), kind=kOutput, calls=%fused_computation.9 | convolution fusion | flops 174325760 | bytes 4096000 | tf_op jit(solution)/shard_map/khij,kjhp->kihp/dot_general | solution.py:86
  192.6 5.4 %multiply_reduce_fusion = (f32[128]{0:T(128)S(1)}, f32[1,128,80,64]{1,3,2,0:T(8,128)}) fusion(f32[1,128,80,64]{1,3,2,0:T(8,128)S(1)} %copy-done.4, f32[1,128,80,64]{1,3,2,0:T(8,128)S(1)} %copy-done.5, f32[80]{0:T(128)S(1)} %copy-done.10, f32[80,64,128]{2,1,0:T(8,128)} %collective-permute-done.2, f32[]{:T(128)} %bitcast.20, ...), kind=kOutput, calls=%fused_computation.23 | convolution fusion | flops 1014497152 | bytes 13181956 | tf_op jit(solution)/shard_map/kin,khpn->kihp/dot_general | solution.py:110
  197.9 3.2 %copy.57 = f32[128,5120]{1,0:T(8,128)} copy(f32[128,5120]{0,1:T(8,128)} %bitcast.104) | data formatting | bytes 5242880 | tf_op jit(solution)/shard_map/reshape | solution.py:114
  201.2 3.8 %fusion.18 = bf16[128,5120]{1,0:T(8,128)(2,1)} fusion(f32[128,5120]{1,0:T(8,128)} %copy.57, f32[5120]{0:T(1024)S(1)} %copy-done.6, f32[128]{0:T(128)S(1)} %add_rsqrt_fusion, bf16[16,8,5120]{2,1,0:T(8,128)(2,1)S(1)} %gather_fusion.7, pred[16]{0:T(512)(128)(4,1)S(1)} %compare_and_fusion), kind=kLoop, calls=%fused_computation.34 | loop fusion | flops 6553600 | bytes 5263888 | tf_op jit(solution)/shard_map/convert_element_type | solution.py:121
  (79 shorter events, 35.2 us)
Async XLA Ops:
  0.0 10.8 %copy-start = (bf16[128,256]{1,0:T(8,128)(2,1)S(1)}, bf16[128,256]{1,0:T(8,128)(2,1)}, u32[]{:S(2)}) copy-start(bf16[128,256]{1,0:T(8,128)(2,1)} %param.14) | copy-start | bytes 196612
  1.8 11.6 %all-to-all-start.1 = ((s32[8,2,1]{1,2,0:T(1,128)}), s32[8,2,1]{1,2,0:T(1,128)S(1)}, u32[]{:S(2)}, u32[]{:S(2)}) async-start(s32[8,2,1]{1,2,0:T(1,128)} %bitcast.1), calls=%async_computation.1 | async-start | bytes 8192 | tf_op jit(solution)/shard_map/all_to_all | solution.py:57
  8.2 1.9 copy-start.7
  13.4 10.3 %all-to-all-start.3 = ((bf16[16,8,80]{2,1,0:T(8,128)(2,1)}), bf16[16,8,80]{2,1,0:T(8,128)(2,1)S(1)}, u32[]{:S(2)}, u32[]{:S(2)}) async-start(bf16[16,8,80]{2,1,0:T(8,128)(2,1)} %broadcast_select_fusion.4), calls=%async_computation.3 | async-start | bytes 65536 | tf_op jit(solution)/shard_map/all_to_all | solution.py:56
  19.9 7.2 %copy-start.3 = (bf16[16,8,5120]{2,1,0:T(8,128)(2,1)S(1)}, bf16[16,8,5120]{2,1,0:T(8,128)(2,1)}, u32[]{:S(2)}) copy-start(bf16[16,8,5120]{2,1,0:T(8,128)(2,1)} %gather_fusion.6) | copy-start | bytes 3932164
  23.8 9.0 %all-to-all-start.2 = ((bf16[16,8,256]{2,1,0:T(8,128)(2,1)}), bf16[16,8,256]{2,1,0:T(8,128)(2,1)S(1)}, u32[]{:S(2)}, u32[]{:S(2)}) async-start(bf16[16,8,256]{2,1,0:T(8,128)(2,1)} %broadcast_select_fusion.3), calls=%async_computation.2 | async-start | bytes 131072 | tf_op jit(solution)/shard_map/all_to_all | solution.py:55
  30.2 6.9 %copy-start.9 = (f32[80]{0:T(128)S(1)}, f32[80]{0:T(128)}, u32[]{:S(2)}) copy-start(f32[80]{0:T(128)} %param.18) | copy-start | bytes 964
  30.2 9.2 %copy-start.8 = (f32[80]{0:T(128)S(1)}, f32[80]{0:T(128)}, u32[]{:S(2)}) copy-start(f32[80]{0:T(128)} %param.19) | copy-start | bytes 964
  32.8 33.3 %all-to-all-start = ((bf16[16,8,5120]{2,1,0:T(8,128)(2,1)}), bf16[16,8,5120]{2,1,0:T(8,128)(2,1)}, u32[]{:S(2)}, u32[]{:S(2)}) async-start(bf16[16,8,5120]{2,1,0:T(8,128)(2,1)} %get-tuple-element.23), calls=%async_computation | async-start | bytes 2621440 | tf_op jit(solution)/shard_map/all_to_all | solution.py:52
  79.7 35.0 %collective-permute-start = (f32[80,64,128]{2,1,0:T(8,128)S(1)}, f32[80,64,128]{2,1,0:T(8,128)S(1)}, u32[]{:S(2)}, u32[]{:S(2)}) collective-permute-start(f32[80,64,128]{2,1,0:T(8,128)S(1)} %get-tuple-element.26), channel_id=1, source_target_pairs={{0,1},{1,2},{2,3},{4,5},{5,6},{6,7},{8,9},{9,10},{10,11},{12,13},{... | collective-permute-start | bytes 7864328 | tf_op jit(solution)/shard_map/ppermute | solution.py:13
  116.6 33.3 %collective-permute-start.1 = (f32[80,64,128]{2,1,0:T(8,128)}, f32[80,64,128]{2,1,0:T(8,128)}, u32[]{:S(2)}, u32[]{:S(2)}) collective-permute-start(f32[80,64,128]{2,1,0:T(8,128)} %multiply_add_fusion.1), channel_id=1, source_target_pairs={{0,1},{1,2},{2,3},{4,5},{5,6},{6,7},{8,9},{9,10},{10,11},{12,13},{... | collective-permute-start | bytes 7864328 | tf_op jit(solution)/shard_map/ppermute | solution.py:13
  121.0 44.9 %all-to-all-start.4 = ((bf16[16,8,5120]{2,1,0:T(8,128)(2,1)}), bf16[16,8,5120]{2,1,0:T(8,128)(2,1)}, u32[]{:S(2)}, u32[]{:S(2)}) async-start(bf16[16,8,5120]{2,1,0:T(8,128)(2,1)} %get-tuple-element.22), calls=%async_computation.4 | async-start | bytes 2621440 | tf_op jit(solution)/shard_map/all_to_all | solution.py:115
  153.5 39.1 %collective-permute-start.2 = (f32[80,64,128]{2,1,0:T(8,128)}, f32[80,64,128]{2,1,0:T(8,128)}, u32[]{:S(2)}, u32[]{:S(2)}) collective-permute-start(f32[80,64,128]{2,1,0:T(8,128)} %multiply_add_fusion), channel_id=1, source_target_pairs={{0,1},{1,2},{2,3},{4,5},{5,6},{6,7},{8,9},{9,10},{10,11},{12,13},{... | collective-permute-start | bytes 7864328 | tf_op jit(solution)/shard_map/ppermute | solution.py:13
  158.4 4.8 %copy-start.2 = (bf16[16,8,5120]{2,1,0:T(8,128)(2,1)S(1)}, bf16[16,8,5120]{2,1,0:T(8,128)(2,1)}, u32[]{:S(2)}) copy-start(bf16[16,8,5120]{2,1,0:T(8,128)(2,1)} %get-tuple-element.12) | copy-start | bytes 3932164
  187.1 5.4 %copy-start.4 = (f32[1,128,80,64]{1,3,2,0:T(8,128)S(1)}, f32[1,128,80,64]{1,3,2,0:T(8,128)}, u32[]{:S(2)}) copy-start(f32[1,128,80,64]{1,3,2,0:T(8,128)} %copy.59) | copy-start | bytes 7864324
  187.1 5.4 %copy-start.5 = (f32[1,128,80,64]{1,3,2,0:T(8,128)S(1)}, f32[1,128,80,64]{1,3,2,0:T(8,128)}, u32[]{:S(2)}) copy-start(f32[1,128,80,64]{1,3,2,0:T(8,128)} %copy.56) | copy-start | bytes 7864324
  187.1 5.4 %copy-start.10 = (f32[80]{0:T(128)S(1)}, f32[80]{0:T(128)}, u32[]{:S(2)}) copy-start(f32[80]{0:T(128)} %param.20) | copy-start | bytes 964
  197.9 3.2 %copy-start.6 = (f32[5120]{0:T(1024)S(1)}, f32[5120]{0:T(1024)}, u32[]{:S(2)}) copy-start(f32[5120]{0:T(1024)} %param.21) | copy-start | bytes 61444
  201.2 3.8 %copy-start.1 = (bf16[128,256]{1,0:T(8,128)(2,1)S(1)}, bf16[128,256]{1,0:T(8,128)(2,1)}, u32[]{:S(2)}) copy-start(bf16[128,256]{1,0:T(8,128)(2,1)} %param.14) | copy-start | bytes 196612
where the time goes:
time: 206 us; the launch traced here: 205 us
  waiting for transfers between devices  76 us (37%)
  local copies, waits for them, and re-layouts  54.6 us (27%)
  starting transfers between devices  38.5 us (19%)
  other arithmetic  21.3 us (10%)
  matrix products  13.6 us (7%)
    ppermute x3, waiting for transfers between devices, passed_along(): return lax.ppermute(block, axis, route)  53.2 us
    all_to_all x1, waiting for transfers between devices, body(): lax.all_to_all(outgoing(signals[:, inner_width:]), 'pack', split_axis=0,...  18.1 us
    ppermute x3, starting transfers between devices, passed_along(): return lax.ppermute(block, axis, route)  15.4 us
    convert_element_type x2, local copies, waits for them, and re-layouts, body(): gated = mixed * jax.nn.silu(gate_in.astype(jnp.float32))  11.3 us
    convert_element_type x2, local copies, waits for them, and re-layouts, body(): inputs.astype(jnp.float32) * to_end[..., None]  10.9 us
    mul x2, local copies, waits for them, and re-layouts, body(): inputs.astype(jnp.float32) * to_end[..., None]  7.54 us
    all_to_all x1, starting transfers between devices, body(): lax.all_to_all(send_slot, 'pack', split_axis=0, concat_axis=0, tiled=True)  6.38 us
    gather x4, local copies, waits for them, and re-layouts, arrange(): jnp.take(values, source_of, axis=0).reshape(token_count, values.shape[-1])  6.08 us
  transfers between devices with their start and end apart: 8, of which 6 were waited for; matrix products, arithmetic and copies ran while one was open for 29% of the time, Pallas kernels for 0%

commit v1 on v0

--- a/solution.py
+++ b/solution.py
@@ -1,10 +1,17 @@
+import functools
+
 import jax
 import jax.numpy as jnp
 from jax import lax
+from jax.experimental import pallas as pl
+from jax.experimental.pallas import tpu as pltpu
 from jax.sharding import PartitionSpec as P
 
 GROUP = 128
 ROW = 8
+CHUNK = 512
+GATE_AFTER = True
+MESH = pl.DeviceIdType.MESH
 
 
 def passed_along(block, axis, distance):
@@ -121,9 +128,335 @@
     return result.astype(jnp.bfloat16)
 
 
+def exact_permute(onehot, values):
+    return jnp.dot(onehot, values, preferred_element_type=jnp.float32).astype(jnp.bfloat16)
+
+
+def split_sum(values):
+    high = values.astype(jnp.bfloat16)
+    low = (values - high.astype(jnp.float32)).astype(jnp.bfloat16)
+    return jnp.concatenate([high, low], axis=1)
+
+
+def fused_kernel(
+    pack_size,
+    ctx_size,
+    head_width,
+    signals,
+    state_io,
+    step_raw,
+    row_target,
+    table_start,
+    log_rate,
+    step_bias,
+    skip_gain,
+    norm_gain,
+    out,
+    order,
+    pieces,
+    small,
+    x_stage,
+    z_stage,
+    x_got,
+    z_got,
+    heads,
+    mixed,
+    grow,
+    local,
+    leave,
+    enter,
+    x_send,
+    x_recv,
+    z_send,
+    z_recv,
+    s_send,
+    s_recv,
+):
+    tokens = GROUP
+    rows = tokens // ROW
+    inner = norm_gain.shape[1]
+    head_count = log_rate.shape[1]
+    width = state_io.shape[1]
+    state = width // 2
+    block = tokens // pack_size
+    chunk = CHUNK
+    chunks = inner // chunk
+    me = lax.axis_index("pack")
+    slab = lax.axis_index("ctx")
+    barrier = pltpu.get_barrier_semaphore()
+    for off in range(1, pack_size):
+        pl.semaphore_signal(
+            barrier, inc=1, device_id={"pack": lax.rem(me + off, pack_size)}, device_id_type=MESH
+        )
+    for off in range(1, ctx_size):
+        pl.semaphore_signal(
+            barrier, inc=1, device_id={"ctx": lax.rem(slab + off, ctx_size)}, device_id_type=MESH
+        )
+
+    lane = lax.broadcasted_iota(jnp.int32, (tokens, tokens), 1)
+    sub = lax.broadcasted_iota(jnp.int32, (tokens, tokens), 0)
+    goal_lane = jnp.zeros((1, tokens), jnp.int32)
+    goal_rows = []
+    slot_rows = []
+    for j in range(rows):
+        target = row_target[j]
+        goal = target // rows
+        goal_lane = jnp.where(lane[:1] // ROW == j, goal, goal_lane)
+        goal_rows.append(jnp.full((ROW, tokens), goal, jnp.int32))
+        slot_rows.append(jnp.full((ROW, tokens), target - goal * rows, jnp.int32))
+    goal_sub = jnp.concatenate(goal_rows, axis=0)
+    slot_sub = jnp.concatenate(slot_rows, axis=0)
+    earlier = (goal_sub == goal_lane) & (sub // ROW < lane // ROW) & (sub % ROW == 0)
+    earlier = jnp.sum(jnp.where(earlier, 1.0, 0.0), axis=0, keepdims=True).astype(jnp.int32)
+    place = (goal_lane * (rows // pack_size) + earlier) * ROW + lane[:1] % ROW
+    send_order = jnp.where(sub == place, 1.0, 0.0).astype(jnp.bfloat16)
+    small[:, :width] = state_io[...]
+    small[:, width : width + 128] = jnp.zeros((tokens, 128), jnp.bfloat16)
+    small[:, width : width + head_count] = step_raw[...]
+    small[:, width + 128 :] = (slot_sub * ROW + sub % ROW).astype(jnp.float32).astype(jnp.bfloat16)
+    x_stage[:, :, inner:] = exact_permute(send_order, small[...]).reshape(
+        pack_size, block, width + 256
+    )
+
+    @pl.loop(0, chunks)
+    def _(c):
+        at = pl.multiple_of(c * chunk, chunk)
+        x_stage[:, :, pl.ds(at, chunk)] = exact_permute(
+            send_order, signals[:, pl.ds(inner + at, chunk)]
+        ).reshape(pack_size, block, chunk)
+
+    pl.semaphore_wait(barrier, pack_size + ctx_size - 2)
+
+    def x_copy(peer, slot):
+        return pltpu.make_async_remote_copy(
+            src_ref=x_stage.at[peer],
+            dst_ref=x_got.at[slot],
+            send_sem=x_send.at[peer],
+            recv_sem=x_recv.at[slot],
+            device_id={"pack": peer},
+            device_id_type=MESH,
+        )
+
+    def z_copy(peer, slot):
+        return pltpu.make_async_remote_copy(
+            src_ref=z_stage.at[peer],
+            dst_ref=z_got.at[slot],
+            send_sem=z_send.at[peer],
+            recv_sem=z_recv.at[slot],
+            device_id={"pack": peer},
+            device_id_type=MESH,
+        )
+
+    def s_copy(c):
+        return pltpu.make_async_remote_copy(
+            src_ref=leave.at[c],
+            dst_ref=enter.at[c],
+            send_sem=s_send.at[c],
+            recv_sem=s_recv.at[c],
+            device_id={"ctx": lax.rem(slab + 1, ctx_size)},
+            device_id_type=MESH,
+        )
+
+    for off in range(1, pack_size):
+        x_copy(lax.rem(me + off, pack_size), me).start()
+
+    @pl.loop(0, chunks)
+    def _(c):
+        at = pl.multiple_of(c * chunk, chunk)
+        z_stage[:, :, pl.ds(at, chunk)] = exact_permute(
+            send_order, signals[:, pl.ds(at, chunk)]
+        ).reshape(pack_size, block, chunk)
+
+    x_got[me] = x_stage[me]
+    z_got[me] = z_stage[me]
+    if GATE_AFTER:
+        for off in range(1, pack_size):
+            x_copy(lax.rem(me + off, pack_size), me).wait_send()
+    for off in range(1, pack_size):
+        z_copy(lax.rem(me + off, pack_size), me).start()
+    for off in range(1, pack_size):
+        peer = lax.rem(me + off, pack_size)
+        x_copy(peer, peer).wait_recv()
+
+    heads[...] = jnp.zeros(heads.shape, jnp.float32)
+    heads[0:1, :head_count] = log_rate[...]
+    heads[1:2, :head_count] = step_bias[...]
+    heads[2:3, :head_count] = skip_gain[...]
+    maps = x_got[:, :, inner : inner + width].reshape(tokens, width)
+    b_map = maps[:, :state]
+    c_map = maps[:, state:]
+    raw = x_got[:, :, inner + width : inner + width + 128].reshape(tokens, 128)
+    spot = x_got[:, :, inner + width + 128 :].reshape(tokens, 128).astype(jnp.float32)
+    spot_lane = spot.T
+    past = spot_lane <= spot
+    order[...] = jnp.where(spot_lane == sub.astype(jnp.float32), 1.0, 0.0).astype(jnp.bfloat16)
+    u = raw.astype(jnp.float32) + heads[1:2, :]
+    dt = jnp.maximum(u, 0.0) + jnp.log(1.0 + jnp.exp(-jnp.abs(u)))
+    a = -jnp.exp(heads[0:1, :]) * dt
+    cum = jnp.dot(
+        jnp.where(past, 1.0, 0.0),
+        a,
+        preferred_element_type=jnp.float32,
+        precision=lax.Precision.HIGHEST,
+    )
+    last = jnp.sum(a, axis=0, keepdims=True)
+    mid = 0.5 * last
+    dots = lax.dot_general(
+        c_map, b_map, (((1,), (1,)), ((), ())), preferred_element_type=jnp.float32
+    )
+    dots = jnp.where(past, dots, 0.0).astype(jnp.bfloat16)
+    b_flip = b_map.astype(jnp.float32).T.astype(jnp.bfloat16)
+    left = jnp.concatenate([dots, b_flip], axis=0)
+    shrink = split_sum(jnp.exp(mid - cum) * dt)
+    rise = split_sum(jnp.exp(cum - mid))
+    keep = (1 - table_start[0]).astype(jnp.float32)
+    half = jnp.exp(mid)
+    vectors = split_sum(
+        jnp.concatenate(
+            [half, keep * half, keep * (half * half), heads[2:3, :], jnp.zeros((4, 128), jnp.float32)],
+            axis=0,
+        )
+    )
+    pieces[0:tokens] = shrink
+    pieces[tokens : 2 * tokens] = rise
+    pieces[2 * tokens : 2 * tokens + 8] = vectors
+    pieces[2 * tokens + 8 :] = jnp.zeros((8, 256), jnp.bfloat16)
+
+    def spread(c, part):
+        head = lax.broadcasted_iota(jnp.int32, (256, chunk), 0) % 128
+        column = lax.broadcasted_iota(jnp.int32, (256, chunk), 1) // head_width
+        pick = jnp.where(head == column + c * (chunk // head_width), 1.0, 0.0)
+        return jnp.dot(part, pick.astype(jnp.bfloat16), preferred_element_type=jnp.float32)
+
+    @pl.loop(0, chunks)
+    def _(c):
+        at = pl.multiple_of(c * chunk, chunk)
+        wide = spread(c, pieces[...])
+        ups = wide[tokens : 2 * tokens]
+        half_wide = wide[2 * tokens : 2 * tokens + 1]
+        x = x_got[:, :, pl.ds(at, chunk)].reshape(tokens, chunk).astype(jnp.float32)
+        scaled = (x * wide[:tokens]).astype(jnp.bfloat16)
+        both = jnp.dot(left, scaled, preferred_element_type=jnp.float32)
+        y = both[:tokens] * ups + wide[2 * tokens + 3 : 2 * tokens + 4] * x
+        mixed[:, :, pl.ds(at, chunk)] = y.reshape(pack_size, block, chunk)
+        leaving = both[tokens:] * half_wide
+
+        @pl.when(slab == 0)
+        def _():
+            leave[c] = leaving.astype(jnp.bfloat16)
+            s_copy(c).start()
+
+        @pl.when(slab > 0)
+        def _():
+            local[c] = leaving
+            grow[c] = ups * wide[2 * tokens + 1 : 2 * tokens + 2]
+
+    @pl.when(slab > 0)
+    def _():
+        @pl.loop(0, chunks)
+        def _(c):
+            at = pl.multiple_of(c * chunk, chunk)
+            decay = spread(c, pieces[2 * tokens :])[2:3]
+            s_copy(c).wait_recv()
+            got = enter[c]
+
+            @pl.when(slab < ctx_size - 1)
+            def _():
+                leave[c] = (decay * got.astype(jnp.float32) + local[c]).astype(jnp.bfloat16)
+                s_copy(c).start()
+
+            carried = jnp.dot(c_map, got, preferred_element_type=jnp.float32) * grow[c]
+            mixed[:, :, pl.ds(at, chunk)] += carried.reshape(pack_size, block, chunk)
+
+    for off in range(pack_size):
+        peer = lax.rem(me + off, pack_size)
+        if off > 0:
+            z_copy(peer, peer).wait_recv()
+        z = z_got[peer].astype(jnp.float32)
+        g = mixed[peer] * (z / (1.0 + jnp.exp(-z)))
+        scale = lax.rsqrt(jnp.mean(g * g, axis=-1, keepdims=True) + 1e-05)
+        out[peer] = (g * scale * norm_gain[...]).astype(jnp.bfloat16)
+
+    for off in range(1, pack_size):
+        peer = lax.rem(me + off, pack_size)
+        if not GATE_AFTER:
+            x_copy(peer, me).wait_send()
+        z_copy(peer, me).wait_send()
+
+    @pl.when(slab < ctx_size - 1)
+    def _():
+        @pl.loop(0, chunks)
+        def _(c):
+            s_copy(c).wait_send()
+
+
+def fused_body(
+    signals, state_io, step_raw, row_target, table_start, log_rate, step_bias, skip_gain, norm_gain
+):
+    pack_size = lax.axis_size("pack")
+    ctx_size = lax.axis_size("ctx")
+    tokens = signals.shape[0]
+    inner = signals.shape[1] // 2
+    width = state_io.shape[1]
+    state = width // 2
+    head_count = log_rate.shape[0]
+    block = tokens // pack_size
+    chunks = inner // CHUNK
+    vmem = pl.BlockSpec(memory_space=pltpu.VMEM)
+    smem = pl.BlockSpec(memory_space=pltpu.SMEM)
+    unsorted, order = pl.pallas_call(
+        functools.partial(fused_kernel, pack_size, ctx_size, inner // head_count),
+        out_shape=(
+            jax.ShapeDtypeStruct((pack_size, block, inner), jnp.bfloat16),
+            jax.ShapeDtypeStruct((tokens, tokens), jnp.bfloat16),
+        ),
+        in_specs=[vmem, vmem, vmem, smem, smem, vmem, vmem, vmem, vmem],
+        out_specs=(vmem, vmem),
+        scratch_shapes=[
+            pltpu.VMEM((2 * tokens + 16, 256), jnp.bfloat16),
+            pltpu.VMEM((tokens, width + 256), jnp.bfloat16),
+            pltpu.VMEM((pack_size, block, inner + width + 256), jnp.bfloat16),
+            pltpu.VMEM((pack_size, block, inner), jnp.bfloat16),
+            pltpu.VMEM((pack_size, block, inner + width + 256), jnp.bfloat16),
+            pltpu.VMEM((pack_size, block, inner), jnp.bfloat16),
+            pltpu.VMEM((8, 128), jnp.float32),
+            pltpu.VMEM((pack_size, block, inner), jnp.float32),
+            pltpu.VMEM((chunks, tokens, CHUNK), jnp.float32),
+            pltpu.VMEM((chunks, state, CHUNK), jnp.float32),
+            pltpu.VMEM((chunks, state, CHUNK), jnp.bfloat16),
+            pltpu.VMEM((chunks, state, CHUNK), jnp.bfloat16),
+            pltpu.SemaphoreType.DMA((pack_size,)),
+            pltpu.SemaphoreType.DMA((pack_size,)),
+            pltpu.SemaphoreType.DMA((pack_size,)),
+            pltpu.SemaphoreType.DMA((pack_size,)),
+            pltpu.SemaphoreType.DMA((chunks,)),
+            pltpu.SemaphoreType.DMA((chunks,)),
+        ],
+        compiler_params=pltpu.CompilerParams(
+            collective_id=0, has_side_effects=True, vmem_limit_bytes=48 * 1024 * 1024
+        ),
+    )(
+        signals,
+        state_io,
+        step_raw,
+        row_target.reshape(-1),
+        table_start.reshape(-1),
+        log_rate.reshape(1, -1),
+        step_bias.reshape(1, -1),
+        skip_gain.reshape(1, -1),
+        norm_gain.reshape(1, -1),
+    )
+    return exact_permute(order, unsorted.reshape(tokens, inner))
+
+
+def either_body(*arguments):
+    one_group = arguments[0].shape[0] == GROUP and arguments[0].shape[1] % (2 * CHUNK) == 0
+    return (fused_body if one_group else body)(*arguments)
+
+
 def solution(mesh):
     return jax.shard_map(
-        body,
+        either_body,
         mesh=mesh,
         in_specs=(
             P(("pack", "ctx"), None),

time: 206 us -> 83 us (0.40)
  the two profiles are of different devices: /device:TPU:1 before, /device:TPU:15 now
where the time goes in v1:
time: 83 us; the launch traced here: 82.7 us
  Pallas kernels  73.7 us (89%)
  local copies, waits for them, and re-layouts  6.76 us (8%)
  matrix products  1.55 us (2%)
    pallas_call x1, Pallas kernels, fused_body(): pl.pallas_call(functools.partial(fused_kernel, pack_size, ctx_size, inner...  73.7 us
    unnamed x15, local copies, waits for them, and re-layouts  6.76 us

profile of v1, /device:TPU:15, one launch (start us, length us, event | category | flops | bytes accessed | tf_op | source)
XLA Modules:
  0.0 82.7 jit_solution(8280595052587083611)
XLA Ops:
  0.7 0.8 %copy.10.step_raw = bf16[128,80]{1,0:T(8,128)(2,1)S(1)} copy(bf16[128,80]{0,1:T(8,128)(2,1)} %param.11) | data formatting | bytes 40960 | tf_op args[2]
  1.5 0.0 copy-start
  1.5 1.7 %copy-done = bf16[128,10240]{1,0:T(8,128)(2,1)S(1)} copy-done((bf16[128,10240]{1,0:T(8,128)(2,1)S(1)}, bf16[128,10240]{1,0:T(8,128)(2,1)}, u32[]{:S(2)}) %copy-start) | copy-done | bytes 2621464
  3.2 0.0 copy-start.1
  3.2 0.8 %copy-done.1 = bf16[128,256]{1,0:T(8,128)(2,1)S(1)} copy-done((bf16[128,256]{1,0:T(8,128)(2,1)S(1)}, bf16[128,256]{1,0:T(8,128)(2,1)}, u32[]{:S(2)}) %copy-start.1) | copy-done | bytes 65560
  4.1 0.0 copy-start.2
  4.1 0.7 copy-done.2
  4.8 0.0 copy-start.3
  4.8 0.7 copy-done.3
  5.5 0.0 copy-start.4
  5.5 0.7 copy-done.4
  6.1 0.0 copy-start.5
  6.1 0.7 copy-done.5
  6.8 0.0 copy-start.6
  6.8 0.7 copy-done.6
  7.4 73.7 %shard_map.91 = (bf16[8,16,5120]{2,1,0:T(8,128)(2,1)S(1)}, bf16[128,128]{1,0:T(8,128)(2,1)S(1)}) custom-call(bf16[128,10240]{1,0:T(8,128)(2,1)S(1)} %copy-done, bf16[128,256]{1,0:T(8,128)(2,1)S(1)} %copy-done.1, bf16[128,80]{1,0:T(8,128)(2,1)S(1)} %copy.10.step_raw, s32[16]{0:T(128)S(1)} %bitcast.12, s32[1]{0:T(128)} %bitcast.9.table_start, ...), custom_call_target="tpu_custom_call" | custom-call | tf_op jit(solution)/shard_map/pallas_call | solution.py:407
  81.1 1.6 %convolution_convert_fusion = bf16[128,5120]{1,0:T(8,128)(2,1)} fusion(bf16[128,128]{1,0:T(8,128)(2,1)S(1)} %get-tuple-element.7, bf16[128,5120]{1,0:T(8,128)(2,1)S(1)} %bitcast.10), kind=kOutput, calls=%fused_computation | convolution fusion | flops 168427520 | bytes 2654208 | tf_op jit(solution)/shard_map/dot_general | solution.py:132
Async XLA Ops:
  1.5 1.8 %copy-start = (bf16[128,10240]{1,0:T(8,128)(2,1)S(1)}, bf16[128,10240]{1,0:T(8,128)(2,1)}, u32[]{:S(2)}) copy-start(bf16[128,10240]{1,0:T(8,128)(2,1)} %signals.1) | copy-start | bytes 7864324
  3.2 0.8 %copy-start.1 = (bf16[128,256]{1,0:T(8,128)(2,1)S(1)}, bf16[128,256]{1,0:T(8,128)(2,1)}, u32[]{:S(2)}) copy-start(bf16[128,256]{1,0:T(8,128)(2,1)} %state_io.1) | copy-start | bytes 196612
  4.1 0.7 copy-start.2
  4.8 0.7 copy-start.3
  5.5 0.7 copy-start.4
  6.1 0.7 copy-start.5
  6.8 0.7 copy-start.6

commit v2 on v1

--- a/solution.py
+++ b/solution.py
@@ -142,18 +142,29 @@
     pack_size,
     ctx_size,
     head_width,
-    signals,
+    signals_hbm,
+    state_io_hbm,
+    step_flip_hbm,
+    row_target_hbm,
+    table_start_hbm,
+    log_rate_hbm,
+    step_bias_hbm,
+    skip_gain_hbm,
+    norm_gain_hbm,
+    out,
+    order,
+    x_in,
+    z_in,
     state_io,
-    step_raw,
+    step_flip,
     row_target,
     table_start,
     log_rate,
     step_bias,
     skip_gain,
     norm_gain,
-    out,
-    order,
     pieces,
+    spacing,
     small,
     x_stage,
     z_stage,
@@ -161,10 +172,9 @@
     z_got,
     heads,
     mixed,
-    grow,
-    local,
     leave,
     enter,
+    load,
     x_send,
     x_recv,
     z_send,
@@ -183,6 +193,25 @@
     chunks = inner // chunk
     me = lax.axis_index("pack")
     slab = lax.axis_index("ctx")
+    loads = [
+        pltpu.make_async_copy(source, held, load.at[i])
+        for i, (source, held) in enumerate(
+            (
+                (row_target_hbm, row_target),
+                (signals_hbm.at[:, pl.ds(inner, inner)], x_in),
+                (state_io_hbm, state_io),
+                (step_flip_hbm, step_flip),
+                (signals_hbm.at[:, pl.ds(0, inner)], z_in),
+                (table_start_hbm, table_start),
+                (log_rate_hbm, log_rate),
+                (step_bias_hbm, step_bias),
+                (skip_gain_hbm, skip_gain),
+                (norm_gain_hbm, norm_gain),
+            )
+        )
+    ]
+    for copy in loads:
+        copy.start()
     barrier = pltpu.get_barrier_semaphore()
     for off in range(1, pack_size):
         pl.semaphore_signal(
@@ -195,6 +224,10 @@
 
     lane = lax.broadcasted_iota(jnp.int32, (tokens, tokens), 1)
     sub = lax.broadcasted_iota(jnp.int32, (tokens, tokens), 0)
+    head = lax.broadcasted_iota(jnp.int32, (256, chunk), 0) % 128
+    column = lax.broadcasted_iota(jnp.int32, (256, chunk), 1) // head_width
+    spacing[...] = head - column
+    loads[0].wait()
     goal_lane = jnp.zeros((1, tokens), jnp.int32)
     goal_rows = []
     slot_rows = []
@@ -210,9 +243,12 @@
     earlier = jnp.sum(jnp.where(earlier, 1.0, 0.0), axis=0, keepdims=True).astype(jnp.int32)
     place = (goal_lane * (rows // pack_size) + earlier) * ROW + lane[:1] % ROW
     send_order = jnp.where(sub == place, 1.0, 0.0).astype(jnp.bfloat16)
+    for copy in loads[1:4]:
+        copy.wait()
     small[:, :width] = state_io[...]
-    small[:, width : width + 128] = jnp.zeros((tokens, 128), jnp.bfloat16)
-    small[:, width : width + head_count] = step_raw[...]
+    heads[...] = jnp.zeros(heads.shape, jnp.float32)
+    heads[:head_count] = step_flip[...].astype(jnp.float32)
+    small[:, width : width + 128] = heads[...].T.astype(jnp.bfloat16)
     small[:, width + 128 :] = (slot_sub * ROW + sub % ROW).astype(jnp.float32).astype(jnp.bfloat16)
     x_stage[:, :, inner:] = exact_permute(send_order, small[...]).reshape(
         pack_size, block, width + 256
@@ -222,7 +258,7 @@
     def _(c):
         at = pl.multiple_of(c * chunk, chunk)
         x_stage[:, :, pl.ds(at, chunk)] = exact_permute(
-            send_order, signals[:, pl.ds(inner + at, chunk)]
+            send_order, x_in[:, pl.ds(at, chunk)]
         ).reshape(pack_size, block, chunk)
 
     pl.semaphore_wait(barrier, pack_size + ctx_size - 2)
@@ -260,11 +296,14 @@
     for off in range(1, pack_size):
         x_copy(lax.rem(me + off, pack_size), me).start()
 
+    for copy in loads[4:]:
+        copy.wait()
+
     @pl.loop(0, chunks)
     def _(c):
         at = pl.multiple_of(c * chunk, chunk)
         z_stage[:, :, pl.ds(at, chunk)] = exact_permute(
-            send_order, signals[:, pl.ds(at, chunk)]
+            send_order, z_in[:, pl.ds(at, chunk)]
         ).reshape(pack_size, block, chunk)
 
     x_got[me] = x_stage[me]
@@ -278,7 +317,7 @@
         peer = lax.rem(me + off, pack_size)
         x_copy(peer, peer).wait_recv()
 
-    heads[...] = jnp.zeros(heads.shape, jnp.float32)
+    heads[0:8] = jnp.zeros((8, 128), jnp.float32)
     heads[0:1, :head_count] = log_rate[...]
     heads[1:2, :head_count] = step_bias[...]
     heads[2:3, :head_count] = skip_gain[...]
@@ -306,14 +345,19 @@
     )
     dots = jnp.where(past, dots, 0.0).astype(jnp.bfloat16)
     b_flip = b_map.astype(jnp.float32).T.astype(jnp.bfloat16)
-    left = jnp.concatenate([dots, b_flip], axis=0)
     shrink = split_sum(jnp.exp(mid - cum) * dt)
     rise = split_sum(jnp.exp(cum - mid))
-    keep = (1 - table_start[0]).astype(jnp.float32)
+    keep = (1 - table_start[0, 0]).astype(jnp.float32)
     half = jnp.exp(mid)
     vectors = split_sum(
         jnp.concatenate(
-            [half, keep * half, keep * (half * half), heads[2:3, :], jnp.zeros((4, 128), jnp.float32)],
+            [
+                half,
+                keep * half,
+                keep * (half * half),
+                heads[2:3, :],
+                jnp.zeros((4, 128), jnp.float32),
+            ],
             axis=0,
         )
     )
@@ -322,50 +366,42 @@
     pieces[2 * tokens : 2 * tokens + 8] = vectors
     pieces[2 * tokens + 8 :] = jnp.zeros((8, 256), jnp.bfloat16)
 
-    def spread(c, part):
-        head = lax.broadcasted_iota(jnp.int32, (256, chunk), 0) % 128
-        column = lax.broadcasted_iota(jnp.int32, (256, chunk), 1) // head_width
-        pick = jnp.where(head == column + c * (chunk // head_width), 1.0, 0.0)
-        return jnp.dot(part, pick.astype(jnp.bfloat16), preferred_element_type=jnp.float32)
-
     @pl.loop(0, chunks)
     def _(c):
         at = pl.multiple_of(c * chunk, chunk)
-        wide = spread(c, pieces[...])
+        pick = jnp.where(spacing[...] == c * (chunk // head_width), 1.0, 0.0)
+        wide = jnp.dot(
+            pieces[...], pick.astype(jnp.bfloat16), preferred_element_type=jnp.float32
+        )
         ups = wide[tokens : 2 * tokens]
-        half_wide = wide[2 * tokens : 2 * tokens + 1]
         x = x_got[:, :, pl.ds(at, chunk)].reshape(tokens, chunk).astype(jnp.float32)
         scaled = (x * wide[:tokens]).astype(jnp.bfloat16)
-        both = jnp.dot(left, scaled, preferred_element_type=jnp.float32)
-        y = both[:tokens] * ups + wide[2 * tokens + 3 : 2 * tokens + 4] * x
-        mixed[:, :, pl.ds(at, chunk)] = y.reshape(pack_size, block, chunk)
-        leaving = both[tokens:] * half_wide
+        leaving = wide[2 * tokens : 2 * tokens + 1] * jnp.dot(
+            b_flip, scaled, preferred_element_type=jnp.float32
+        )
 
         @pl.when(slab == 0)
         def _():
             leave[c] = leaving.astype(jnp.bfloat16)
             s_copy(c).start()
 
+        y = jnp.dot(dots, scaled, preferred_element_type=jnp.float32) * ups
+        y += wide[2 * tokens + 3 : 2 * tokens + 4] * x
+        mixed[:, :, pl.ds(at, chunk)] = y.reshape(pack_size, block, chunk)
+
         @pl.when(slab > 0)
         def _():
-            local[c] = leaving
-            grow[c] = ups * wide[2 * tokens + 1 : 2 * tokens + 2]
-
-    @pl.when(slab > 0)
-    def _():
-        @pl.loop(0, chunks)
-        def _(c):
-            at = pl.multiple_of(c * chunk, chunk)
-            decay = spread(c, pieces[2 * tokens :])[2:3]
             s_copy(c).wait_recv()
             got = enter[c]
 
             @pl.when(slab < ctx_size - 1)
             def _():
-                leave[c] = (decay * got.astype(jnp.float32) + local[c]).astype(jnp.bfloat16)
+                decay = wide[2 * tokens + 2 : 2 * tokens + 3]
+                leave[c] = (decay * got.astype(jnp.float32) + leaving).astype(jnp.bfloat16)
                 s_copy(c).start()
 
-            carried = jnp.dot(c_map, got, preferred_element_type=jnp.float32) * grow[c]
+            carried = jnp.dot(c_map, got, preferred_element_type=jnp.float32)
+            carried *= ups * wide[2 * tokens + 1 : 2 * tokens + 2]
             mixed[:, :, pl.ds(at, chunk)] += carried.reshape(pack_size, block, chunk)
 
     for off in range(pack_size):
@@ -403,28 +439,38 @@
     block = tokens // pack_size
     chunks = inner // CHUNK
     vmem = pl.BlockSpec(memory_space=pltpu.VMEM)
-    smem = pl.BlockSpec(memory_space=pltpu.SMEM)
+    hbm = pl.BlockSpec(memory_space=pltpu.HBM)
     unsorted, order = pl.pallas_call(
         functools.partial(fused_kernel, pack_size, ctx_size, inner // head_count),
         out_shape=(
             jax.ShapeDtypeStruct((pack_size, block, inner), jnp.bfloat16),
             jax.ShapeDtypeStruct((tokens, tokens), jnp.bfloat16),
         ),
-        in_specs=[vmem, vmem, vmem, smem, smem, vmem, vmem, vmem, vmem],
+        in_specs=[hbm] * 9,
         out_specs=(vmem, vmem),
         scratch_shapes=[
+            pltpu.VMEM((tokens, inner), jnp.bfloat16),
+            pltpu.VMEM((tokens, inner), jnp.bfloat16),
+            pltpu.VMEM((tokens, width), jnp.bfloat16),
+            pltpu.VMEM((head_count, tokens), jnp.bfloat16),
+            pltpu.SMEM((tokens // ROW,), jnp.int32),
+            pltpu.SMEM((1, 1), jnp.int32),
+            pltpu.VMEM((1, head_count), jnp.float32),
+            pltpu.VMEM((1, head_count), jnp.float32),
+            pltpu.VMEM((1, head_count), jnp.float32),
+            pltpu.VMEM((1, inner), jnp.float32),
             pltpu.VMEM((2 * tokens + 16, 256), jnp.bfloat16),
+            pltpu.VMEM((256, CHUNK), jnp.int32),
             pltpu.VMEM((tokens, width + 256), jnp.bfloat16),
             pltpu.VMEM((pack_size, block, inner + width + 256), jnp.bfloat16),
             pltpu.VMEM((pack_size, block, inner), jnp.bfloat16),
             pltpu.VMEM((pack_size, block, inner + width + 256), jnp.bfloat16),
             pltpu.VMEM((pack_size, block, inner), jnp.bfloat16),
-            pltpu.VMEM((8, 128), jnp.float32),
+            pltpu.VMEM((128, tokens), jnp.float32),
             pltpu.VMEM((pack_size, block, inner), jnp.float32),
-            pltpu.VMEM((chunks, tokens, CHUNK), jnp.float32),
-            pltpu.VMEM((chunks, state, CHUNK), jnp.float32),
             pltpu.VMEM((chunks, state, CHUNK), jnp.bfloat16),
             pltpu.VMEM((chunks, state, CHUNK), jnp.bfloat16),
+            pltpu.SemaphoreType.DMA((10,)),
             pltpu.SemaphoreType.DMA((pack_size,)),
             pltpu.SemaphoreType.DMA((pack_size,)),
             pltpu.SemaphoreType.DMA((pack_size,)),
@@ -433,14 +479,14 @@
             pltpu.SemaphoreType.DMA((chunks,)),
         ],
         compiler_params=pltpu.CompilerParams(
-            collective_id=0, has_side_effects=True, vmem_limit_bytes=48 * 1024 * 1024
+            collective_id=0, has_side_effects=True, vmem_limit_bytes=60 * 1024 * 1024
         ),
     )(
         signals,
         state_io,
-        step_raw,
+        step_raw.T,
         row_target.reshape(-1),
-        table_start.reshape(-1),
+        table_start,
         log_rate.reshape(1, -1),
         step_bias.reshape(1, -1),
         skip_gain.reshape(1, -1),

time: 83 us -> 77.3 us (0.931)
  local copies, waits for them, and re-layouts: 6.76 us -> 0 us
  matrix products: 1.55 us -> 2.89 us
    unnamed x15 -> x0, local copies, waits for them, and re-layouts: 6.76 us -> none
    dot_general x1, matrix products: 1.55 us -> 2.89 us  [exact_permute(): jnp.dot(onehot, values, preferred_element_type=jnp.float32)]
where the time goes in v2:
time: 77.3 us; the launch traced here: 77.1 us
  Pallas kernels  73.6 us (95%)
  matrix products  2.89 us (4%)
    pallas_call x1, Pallas kernels, fused_body(): pl.pallas_call(functools.partial(fused_kernel, pack_size, ctx_size, inner...  73.6 us
    dot_general x1, matrix products, exact_permute(): jnp.dot(onehot, values, preferred_element_type=jnp.float32)  2.89 us

profile of v2, /device:TPU:15, one launch (start us, length us, event | category | flops | bytes accessed | tf_op | source)
XLA Modules:
  0.0 77.1 jit_solution(17459468020773233195)
XLA Ops:
  0.7 73.6 %shard_map.91 = (bf16[8,16,5120]{2,1,0:T(8,128)(2,1)}, bf16[128,128]{1,0:T(8,128)(2,1)}) custom-call(bf16[128,10240]{1,0:T(8,128)(2,1)} %signals_hbm.1, bf16[128,256]{1,0:T(8,128)(2,1)} %state_io_hbm.1, bf16[80,128]{1,0:T(8,128)(2,1)} %bitcast.10, s32[16]{0:T(128)} %bitcast.12, s32[1,1]{1,0:T(1,128)S(6)} %copy.10.table_start_hbm, f32[1,80]{1,0:T(1,128)} %bitcast.13, ...), custom_call_target="tpu_custom_call" | custom-call | tf_op jit(solution)/shard_map/pallas_call | solution.py:443
  74.2 2.9 %convolution_convert_fusion = bf16[128,5120]{1,0:T(8,128)(2,1)} fusion(bf16[128,128]{1,0:T(8,128)(2,1)} %get-tuple-element.7, bf16[128,5120]{1,0:T(8,128)(2,1)} %bitcast.9), kind=kOutput, calls=%fused_computation | convolution fusion | flops 168427520 | bytes 2654208 | tf_op jit(solution)/shard_map/dot_general | solution.py:132

commit v3 on v2

--- a/solution.py
+++ b/solution.py
@@ -250,25 +250,25 @@
     heads[:head_count] = step_flip[...].astype(jnp.float32)
     small[:, width : width + 128] = heads[...].T.astype(jnp.bfloat16)
     small[:, width + 128 :] = (slot_sub * ROW + sub % ROW).astype(jnp.float32).astype(jnp.bfloat16)
-    x_stage[:, :, inner:] = exact_permute(send_order, small[...]).reshape(
-        pack_size, block, width + 256
-    )
-
-    @pl.loop(0, chunks)
-    def _(c):
+    half_chunks = chunks // 2
+    cut = half_chunks * chunk
+
+    def stage_x(c):
         at = pl.multiple_of(c * chunk, chunk)
         x_stage[:, :, pl.ds(at, chunk)] = exact_permute(
             send_order, x_in[:, pl.ds(at, chunk)]
         ).reshape(pack_size, block, chunk)
 
+    pl.loop(0, half_chunks)(stage_x)
     pl.semaphore_wait(barrier, pack_size + ctx_size - 2)
 
-    def x_copy(peer, slot):
+    def x_copy(peer, slot, part):
+        columns = pl.ds(0, cut) if part == 0 else pl.ds(cut, x_stage.shape[2] - cut)
         return pltpu.make_async_remote_copy(
-            src_ref=x_stage.at[peer],
-            dst_ref=x_got.at[slot],
-            send_sem=x_send.at[peer],
-            recv_sem=x_recv.at[slot],
+            src_ref=x_stage.at[peer, :, columns],
+            dst_ref=x_got.at[slot, :, columns],
+            send_sem=x_send.at[part, peer],
+            recv_sem=x_recv.at[part, slot],
             device_id={"pack": peer},
             device_id_type=MESH,
         )
@@ -294,7 +294,14 @@
         )
 
     for off in range(1, pack_size):
-        x_copy(lax.rem(me + off, pack_size), me).start()
+        x_copy(lax.rem(me + off, pack_size), me, 0).start()
+    x_stage[:, :, inner:] = exact_permute(send_order, small[...]).reshape(
+        pack_size, block, width + 256
+    )
+
+    pl.loop(half_chunks, chunks)(stage_x)
+    for off in range(1, pack_size):
+        x_copy(lax.rem(me + off, pack_size), me, 1).start()
 
     for copy in loads[4:]:
         copy.wait()
@@ -310,12 +317,14 @@
     z_got[me] = z_stage[me]
     if GATE_AFTER:
         for off in range(1, pack_size):
-            x_copy(lax.rem(me + off, pack_size), me).wait_send()
+            for part in range(2):
+                x_copy(lax.rem(me + off, pack_size), me, part).wait_send()
     for off in range(1, pack_size):
         z_copy(lax.rem(me + off, pack_size), me).start()
     for off in range(1, pack_size):
         peer = lax.rem(me + off, pack_size)
-        x_copy(peer, peer).wait_recv()
+        for part in range(2):
+            x_copy(peer, peer, part).wait_recv()
 
     heads[0:8] = jnp.zeros((8, 128), jnp.float32)
     heads[0:1, :head_count] = log_rate[...]
@@ -416,7 +425,8 @@
     for off in range(1, pack_size):
         peer = lax.rem(me + off, pack_size)
         if not GATE_AFTER:
-            x_copy(peer, me).wait_send()
+            for part in range(2):
+                x_copy(peer, me, part).wait_send()
         z_copy(peer, me).wait_send()
 
     @pl.when(slab < ctx_size - 1)
@@ -471,8 +481,8 @@
             pltpu.VMEM((chunks, state, CHUNK), jnp.bfloat16),
             pltpu.VMEM((chunks, state, CHUNK), jnp.bfloat16),
             pltpu.SemaphoreType.DMA((10,)),
-            pltpu.SemaphoreType.DMA((pack_size,)),
-            pltpu.SemaphoreType.DMA((pack_size,)),
+            pltpu.SemaphoreType.DMA((2, pack_size)),
+            pltpu.SemaphoreType.DMA((2, pack_size)),
             pltpu.SemaphoreType.DMA((pack_size,)),
             pltpu.SemaphoreType.DMA((pack_size,)),
             pltpu.SemaphoreType.DMA((chunks,)),

time: 77.3 us -> 76.8 us (level)
  no operation moved by 1% of the time
where the time goes in v3:
time: 76.8 us; the launch traced here: 76.4 us
  Pallas kernels  72.9 us (95%)
  matrix products  2.89 us (4%)
    pallas_call x1, Pallas kernels, fused_body(): pl.pallas_call(functools.partial(fused_kernel, pack_size, ctx_size, inner...  72.9 us
    dot_general x1, matrix products, exact_permute(): jnp.dot(onehot, values, preferred_element_type=jnp.float32)  2.89 us

profile of v3, /device:TPU:15, one launch (start us, length us, event | category | flops | bytes accessed | tf_op | source)
XLA Modules:
  0.0 76.4 jit_solution(15181590199603959532)
XLA Ops:
  0.7 72.9 %shard_map.91 = (bf16[8,16,5120]{2,1,0:T(8,128)(2,1)}, bf16[128,128]{1,0:T(8,128)(2,1)}) custom-call(bf16[128,10240]{1,0:T(8,128)(2,1)} %signals_hbm.1, bf16[128,256]{1,0:T(8,128)(2,1)} %state_io_hbm.1, bf16[80,128]{1,0:T(8,128)(2,1)} %bitcast.10, s32[16]{0:T(128)} %bitcast.12, s32[1,1]{1,0:T(1,128)S(6)} %copy.10.table_start_hbm, f32[1,80]{1,0:T(1,128)} %bitcast.13, ...), custom_call_target="tpu_custom_call" | custom-call | tf_op jit(solution)/shard_map/pallas_call | solution.py:453
  73.5 2.9 %convolution_convert_fusion = bf16[128,5120]{1,0:T(8,128)(2,1)} fusion(bf16[128,128]{1,0:T(8,128)(2,1)} %get-tuple-element.7, bf16[128,5120]{1,0:T(8,128)(2,1)} %bitcast.9), kind=kOutput, calls=%fused_computation | convolution fusion | flops 168427520 | bytes 2654208 | tf_op jit(solution)/shard_map/dot_general | solution.py:132

commit v4 on v3

--- a/solution.py
+++ b/solution.py
@@ -174,7 +174,9 @@
     mixed,
     leave,
     enter,
+    finished,
     load,
+    store,
     x_send,
     x_recv,
     z_send,
@@ -420,7 +422,8 @@
         z = z_got[peer].astype(jnp.float32)
         g = mixed[peer] * (z / (1.0 + jnp.exp(-z)))
         scale = lax.rsqrt(jnp.mean(g * g, axis=-1, keepdims=True) + 1e-05)
-        out[peer] = (g * scale * norm_gain[...]).astype(jnp.bfloat16)
+        finished[peer] = (g * scale * norm_gain[...]).astype(jnp.bfloat16)
+        pltpu.make_async_copy(finished.at[peer], out.at[peer], store.at[peer]).start()
 
     for off in range(1, pack_size):
         peer = lax.rem(me + off, pack_size)
@@ -428,6 +431,9 @@
             for part in range(2):
                 x_copy(peer, me, part).wait_send()
         z_copy(peer, me).wait_send()
+    for off in range(pack_size):
+        peer = lax.rem(me + off, pack_size)
+        pltpu.make_async_copy(finished.at[peer], out.at[peer], store.at[peer]).wait()
 
     @pl.when(slab < ctx_size - 1)
     def _():
@@ -457,7 +463,7 @@
             jax.ShapeDtypeStruct((tokens, tokens), jnp.bfloat16),
         ),
         in_specs=[hbm] * 9,
-        out_specs=(vmem, vmem),
+        out_specs=(hbm, vmem),
         scratch_shapes=[
             pltpu.VMEM((tokens, inner), jnp.bfloat16),
             pltpu.VMEM((tokens, inner), jnp.bfloat16),
@@ -480,7 +486,9 @@
             pltpu.VMEM((pack_size, block, inner), jnp.float32),
             pltpu.VMEM((chunks, state, CHUNK), jnp.bfloat16),
             pltpu.VMEM((chunks, state, CHUNK), jnp.bfloat16),
+            pltpu.VMEM((pack_size, block, inner), jnp.bfloat16),
             pltpu.SemaphoreType.DMA((10,)),
+            pltpu.SemaphoreType.DMA((pack_size,)),
             pltpu.SemaphoreType.DMA((2, pack_size)),
             pltpu.SemaphoreType.DMA((2, pack_size)),
             pltpu.SemaphoreType.DMA((pack_size,)),

time: 76.8 us -> 77.1 us (level)
  no operation moved by 1% of the time
where the time goes in v4:
time: 77.1 us; the launch traced here: 76.7 us
  Pallas kernels  73.1 us (95%)
  matrix products  2.89 us (4%)
    pallas_call x1, Pallas kernels, fused_body(): pl.pallas_call(functools.partial(fused_kernel, pack_size, ctx_size, inner...  73.1 us
    dot_general x1, matrix products, exact_permute(): jnp.dot(onehot, values, preferred_element_type=jnp.float32)  2.89 us

profile of v4, /device:TPU:15, one launch (start us, length us, event | category | flops | bytes accessed | tf_op | source)
XLA Modules:
  0.0 76.7 jit_solution(15751508105559964002)
XLA Ops:
  0.7 73.1 %shard_map.91 = (bf16[8,16,5120]{2,1,0:T(8,128)(2,1)}, bf16[128,128]{1,0:T(8,128)(2,1)}) custom-call(bf16[128,10240]{1,0:T(8,128)(2,1)} %signals_hbm.1, bf16[128,256]{1,0:T(8,128)(2,1)} %state_io_hbm.1, bf16[80,128]{1,0:T(8,128)(2,1)} %bitcast.10, s32[16]{0:T(128)} %bitcast.12, s32[1,1]{1,0:T(1,128)S(6)} %copy.10.table_start_hbm, f32[1,80]{1,0:T(1,128)} %bitcast.13, ...), custom_call_target="tpu_custom_call" | custom-call | tf_op jit(solution)/shard_map/pallas_call | solution.py:459
  73.8 2.9 %convolution_convert_fusion = bf16[128,5120]{1,0:T(8,128)(2,1)} fusion(bf16[128,128]{1,0:T(8,128)(2,1)} %get-tuple-element.7, bf16[128,5120]{1,0:T(8,128)(2,1)} %bitcast.9), kind=kOutput, calls=%fused_computation | convolution fusion | flops 168427520 | bytes 2654208 | tf_op jit(solution)/shard_map/dot_general | solution.py:132
